TPU v7x, 256 devices: a whole 4x4x8 slice. The times are simulated.
256 devices in a mesh: sub: 32 (over x, z), vec: 8 (over y, core).
Axes of the slice: x: 4, y: 4, z: 8, core: 2. Of those that a mesh axis runs over, the one named last changes fastest.
Arguments:
- coefficients: bfloat16 [1024, 20480], P('sub', 'vec'), may hold values from -6 to 6
- row_counts: int32 [32], replicated, may hold values from 1 to 1024, 16384 in all
- ancestors: int32 [32, 3], replicated, may hold values from 0 to 27, as said below
- interior_modes: bfloat16 [131072, 1024], P('sub'), may hold values from -0.25 to 0.25
- separator_modes: bfloat16 [8192, 128], replicated, may hold values from -0.5 to 0.5
- coupling: bfloat16 [131072, 768], P('sub'), may hold values from -0.3125 to 0.3125
- pattern: int32 [32, 16, 3], P('sub'), may hold values 0 or 1
Outputs:
- interior_field: bfloat16 [131072, 1024], P('sub', 'vec')
- separator_field: bfloat16 [8192, 1024], P('sub', 'vec')
Inputs may be any that keep to these rules, and one draw needn't show every extreme that they name: `ancestors`: the separators form binary trees: substructures pair under level-1 separators, pairs of those under level-2 separators, and so on, so that a level-l separator lies over 2**l substructures; no separator appears at two levels. `row_counts`: the counts sum to 512 * 32.
All inputs are finite; a program needn't handle non-finite values. No bound on the sum of `pattern` on one device may be relied on, other than what follows from the above.
Results may differ from a plain program's by a relative error of at most 0.0038.
Values may be sent and summed in bfloat16 or wider, within the bound.
A program may use at most 128 MiB of HBM per device.

v0:
```python
import jax
import jax.numpy as jnp
from jax import lax
from jax.sharding import PartitionSpec as P

BW = 256
SEPM = 128
LEVELS = 3


def window_rows(full_rows, row_counts, interior_total, cap_rows):
    slice_cols = full_rows.shape[0]
    block_total = interior_total // cap_rows + 1
    padded = jnp.concatenate(
        [full_rows[:, :interior_total], jnp.zeros((slice_cols, cap_rows), full_rows.dtype)], axis=1
    )
    blocks = padded.reshape(slice_cols, block_total, cap_rows)
    offsets = jnp.cumsum(row_counts) - row_counts
    first_block = offsets // cap_rows
    remainder = offsets - first_block * cap_rows
    labels = jnp.arange(block_total, dtype=jnp.int32)
    pick_first = (first_block[:, None] == labels[None, :]).astype(blocks.dtype)
    pick_second = (first_block[:, None] + 1 == labels[None, :]).astype(blocks.dtype)
    lower = jnp.einsum("ob,cbj->ocj", pick_first, blocks, preferred_element_type=jnp.float32)
    upper = jnp.einsum("ob,cbj->ocj", pick_second, blocks, preferred_element_type=jnp.float32)
    window = jnp.concatenate([lower, upper], axis=2).astype(blocks.dtype)
    for bit in range(cap_rows.bit_length() - 1):
        amount = 1 << bit
        moved = jnp.concatenate(
            [window[:, :, amount:], jnp.zeros(window.shape[:2] + (amount,), window.dtype)], axis=2
        )
        flag = remainder >> bit & 1 == 1
        window = jnp.where(flag[:, None, None], moved, window)
    window = window[:, :, :cap_rows]
    positions = jnp.arange(cap_rows, dtype=jnp.int32)
    live = positions[None, :] < row_counts[:, None]
    window = jnp.where(live[:, None, :], window, jnp.zeros((), window.dtype))
    return jnp.transpose(window, (1, 0, 2))


def body(coefficients, row_counts, ancestors, interior_modes, separator_modes, coupling, pattern):
    sub_count = lax.axis_size("sub")
    vec_count = lax.axis_size("vec")
    my_index = lax.axis_index("sub")
    slice_cols = coefficients.shape[0] // vec_count
    rows_vec = coefficients.shape[1]
    regrouped = coefficients.reshape(vec_count, slice_cols, rows_vec)
    full_rows = lax.all_to_all(regrouped, "vec", split_axis=0, concat_axis=2, tiled=True)
    full_rows = full_rows.reshape(slice_cols, vec_count * rows_vec)
    total_rows = full_rows.shape[1]
    interior_total = total_rows - sub_count * SEPM
    cap_rows = interior_modes.shape[1]
    interior_part = window_rows(full_rows, row_counts, interior_total, cap_rows)
    sep_part = full_rows[:, interior_total:].reshape(slice_cols, sub_count, SEPM)
    parts = [interior_part, sep_part]
    picked = jnp.concatenate(parts, axis=2)
    slot_width = picked.shape[2]
    received = lax.all_to_all(picked, "sub", split_axis=1, concat_axis=0, tiled=True)
    group_cols = sub_count * slice_cols
    received = received.reshape(group_cols, slot_width)
    interior_coef = received[:, :cap_rows]
    own_coef = received[:, cap_rows : cap_rows + SEPM]
    modes_by_sep = separator_modes.reshape(sub_count, BW, SEPM)
    own_modes = lax.dynamic_index_in_dim(modes_by_sep, my_index, 0, keepdims=False)
    contract = (((1,), (1,)), ((), ()))
    own_field = lax.dot_general(
        own_modes, own_coef, contract, preferred_element_type=jnp.float32
    ).astype(jnp.bfloat16)
    interior_sum = lax.dot_general(
        interior_modes, interior_coef, contract, preferred_element_type=jnp.float32
    )
    my_ancestors = lax.dynamic_index_in_dim(ancestors, my_index, 0, keepdims=False)
    piece = lax.all_gather(own_field[None], "sub", axis=0, tiled=True)
    labels = jnp.arange(piece.shape[0], dtype=jnp.int32)
    select = (my_ancestors[:, None] == labels[None, :]).astype(piece.dtype)
    ancestor_blocks = jnp.einsum(
        "lc,cbk->lbk", select, piece, preferred_element_type=jnp.float32
    ).astype(jnp.bfloat16)
    block_count = coupling.shape[0] // BW
    gates = pattern[0].astype(coupling.dtype)
    masked = (coupling.reshape(block_count, BW, LEVELS, BW) * gates[:, None, :, None]).reshape(
        coupling.shape
    )
    interior_sum = interior_sum + jnp.dot(
        masked, ancestor_blocks.reshape(LEVELS * BW, group_cols), preferred_element_type=jnp.float32
    )
    return (interior_sum.astype(jnp.bfloat16), own_field)


def solution(mesh):
    placed = (P("sub", "vec"), P(), P(), P("sub", None), P(), P("sub", None), P("sub", None, None))
    return jax.shard_map(
        body,
        mesh=mesh,
        in_specs=placed,
        out_specs=(P("sub", "vec"), P("sub", "vec")),
        check_vma=False,
    )
```

profile of v0, /device:TPU:8, one launch (start us, length us, event | category | flops | bytes accessed | tf_op | source)
XLA Modules:
  0.0 143.3 jit_solution(3298135842300496320)
XLA Ops:
  7.2 0.0 copy-start
  7.2 1.8 %reshape.96 = bf16[8,4,2560]{2,1,0:T(4,128)(2,1)} reshape(bf16[32,2560]{1,0:T(8,128)(2,1)} %param.7) | data formatting | bytes 327680 | tf_op jit(solution)/shard_map/reshape | solution.py:47
  9.0 5.4 %all-to-all-start = ((bf16[8,4,2560]{2,1,0:T(4,128)(2,1)}), bf16[8,4,2560]{2,1,0:T(4,128)(2,1)S(1)}, u32[]{:S(2)}, u32[]{:S(2)}) async-start(bf16[8,4,2560]{2,1,0:T(4,128)(2,1)} %reshape.96), calls=%async_computation | async-start | bytes 327680 | tf_op jit(solution)/shard_map/all_to_all | solution.py:48
  14.4 0.7 iota_compare_fusion
  15.1 0.7 copy.21
  15.9 0.1 reduce-window.9
  15.9 0.1 reduce
  16.1 0.7 and_compare_fusion.9
  16.8 2.7 %all-to-all-done = bf16[8,4,2560]{2,1,0:T(4,128)(2,1)S(1)} async-done(((bf16[8,4,2560]{2,1,0:T(4,128)(2,1)}), bf16[8,4,2560]{2,1,0:T(4,128)(2,1)S(1)}, u32[]{:S(2)}, u32[]{:S(2)}) %all-to-all-start) | async-done | bytes 163872 | tf_op jit(solution)/shard_map/all_to_all | solution.py:48
  19.4 0.8 slice_select_fusion.1
  20.3 0.1 reshape.98
  20.4 0.3 convolution_convert_fusion.1
  20.7 0.3 convolution_convert_fusion
  20.9 0.2 fusion.9
  21.2 0.2 fusion.10
  21.4 0.2 slice.64
  21.6 0.2 pad_select_fusion.7
  21.8 0.2 slice.65
  22.0 0.2 pad_select_fusion.6
  22.2 0.2 slice.66
  22.4 0.2 pad_select_fusion.5
  22.7 0.2 slice.67
  22.9 0.2 pad_select_fusion.4
  23.1 0.2 slice.68
  23.3 0.2 pad_select_fusion.3
  23.5 0.0 copy-start.1
  23.5 0.2 slice.69
  23.7 0.2 pad_select_fusion.2
  24.0 0.2 pad_select_fusion.1
  24.2 0.2 pad_select_fusion
  24.5 0.2 fusion.13
  24.7 0.9 copy.22
  25.5 10.7 %all-to-all-start.1 = ((bf16[4,32,1152]{2,0,1:T(4,128)(2,1)}), bf16[4,32,1152]{2,0,1:T(4,128)(2,1)S(1)}, u32[]{:S(2)}, u32[]{:S(2)}) async-start(bf16[4,32,1152]{2,0,1:T(4,128)(2,1)} %copy.22), calls=%async_computation.1 | async-start | bytes 589824 | tf_op jit(solution)/shard_map/all_to_all | solution.py:58
  36.3 0.2 all-gather.3.cloned.1.call-start
  36.5 12.5 %all-to-all-done.1 = bf16[4,32,1152]{2,0,1:T(4,128)(2,1)S(1)} async-done(((bf16[4,32,1152]{2,0,1:T(4,128)(2,1)}), bf16[4,32,1152]{2,0,1:T(4,128)(2,1)S(1)}, u32[]{:S(2)}, u32[]{:S(2)}) %all-to-all-start.1) | async-done | bytes 294944 | tf_op jit(solution)/shard_map/all_to_all | solution.py:58
  49.0 0.1 reshape.100
  49.1 0.8 convolution_convert_fusion.2
  49.9 0.0 all-gather.3.cloned.1.call-update
  49.9 0.2 dynamic-slice_reduce_fusion
  50.1 0.5 mul.16
  50.6 6.8 %copy.31 = bf16[96,8,16,256]{3,1,2,0:T(8,128)(2,1)} copy(bf16[96,8,16,256]{3,2,1,0:T(8,128)(2,1)S(1)} %bitcast.53) | data formatting | bytes 12582912
  57.5 8.8 %copy.23 = bf16[4096,768]{0,1:T(8,128)(2,1)} copy(bf16[4096,768]{1,0:T(8,128)(2,1)} %param.12) | data formatting | bytes 12582912 | tf_op args[5]
  66.2 56.9 %all-gather.3.cloned.1.call-done = bf16[8192,128]{1,0:T(8,128)(2,1)} async-done(((bf16[256,128]{1,0:T(8,128)(2,1)}), bf16[8192,128]{1,0:T(8,128)(2,1)}) %all-gather.3.cloned.1.call-update) | async-done | bytes 2097168 | tf_op jit(solution)/shard_map/all_gather | solution.py:73
  123.1 3.0 %fusion.6 = bf16[3,256,128]{2,0,1:T(4,128)(2,1)S(1)} fusion(bf16[32,256,128]{2,1,0:T(8,128)(2,1)} %bitcast.56, s32[3]{0:T(128)S(1)} %dynamic-slice_reduce_fusion), kind=kOutput, calls=%fused_computation.9 | convolution fusion | flops 6389856 | bytes 2293772 | tf_op jit(solution)/shard_map/lc,cbk->lbk/dot_general | solution.py:76
  126.1 0.0 slice-start.1
  126.1 6.1 %fusion = f32[4096,128]{0,1:T(8,128)S(1)} fusion(bf16[768,128]{1,0:T(8,128)(2,1)S(1)} %bitcast.58, bf16[4096,768]{0,1:T(8,128)(2,1)} %copy.23, bf16[4096,768]{0,1:T(8,128)(2,1)} %bitcast.52), kind=kOutput, calls=%fused_computation | convolution fusion | flops 808452096 | bytes 14876672 | tf_op jit(solution)/shard_map/dot_general | solution.py:84
  132.2 2.9 %fusion.3 = bf16[4096,128]{0,1:T(8,128)(2,1)S(1)} fusion(f32[4096,128]{0,1:T(8,128)S(1)} %fusion, bf16[4096,1024]{1,0:T(8,128)(2,1)S(1)} %bitcast.55, bf16[128,1152]{1,0:T(8,128)(2,1)S(1)} %reshape.100), kind=kOutput, calls=%fused_computation.4 | convolution fusion | flops 1074790400 | bytes 11796480 | tf_op jit(solution)/shard_map/dot_general | solution.py:69
  135.1 1.3 copy.27
  (19 shorter events, 0.2 us)
Async XLA Ops:
  7.2 41.9 %copy-start = (bf16[8192,128]{1,0:T(8,128)(2,1)S(1)}, bf16[8192,128]{1,0:T(8,128)(2,1)}, u32[]{:S(2)}) copy-start(bf16[8192,128]{1,0:T(8,128)(2,1)} %param.11) | copy-start | bytes 6291460
  9.0 10.5 %all-to-all-start = ((bf16[8,4,2560]{2,1,0:T(4,128)(2,1)}), bf16[8,4,2560]{2,1,0:T(4,128)(2,1)S(1)}, u32[]{:S(2)}, u32[]{:S(2)}) async-start(bf16[8,4,2560]{2,1,0:T(4,128)(2,1)} %reshape.96), calls=%async_computation | async-start | bytes 327680 | tf_op jit(solution)/shard_map/all_to_all | solution.py:48
  23.5 26.4 %copy-start.1 = (s32[32,3]{0,1:T(4,128)S(1)}, s32[32,3]{0,1:T(4,128)}, u32[]{:S(2)}) copy-start(s32[32,3]{0,1:T(4,128)} %param.9) | copy-start | bytes 1156
  23.5 26.6 %copy-start.2 = (s32[1,16,3]{1,0,2:T(1,128)S(1)}, s32[1,16,3]{1,0,2:T(1,128)}, u32[]{:S(2)}) copy-start(s32[1,16,3]{1,0,2:T(1,128)} %param.13) | copy-start | bytes 580
  25.5 23.5 %all-to-all-start.1 = ((bf16[4,32,1152]{2,0,1:T(4,128)(2,1)}), bf16[4,32,1152]{2,0,1:T(4,128)(2,1)S(1)}, u32[]{:S(2)}, u32[]{:S(2)}) async-start(bf16[4,32,1152]{2,0,1:T(4,128)(2,1)} %copy.22), calls=%async_computation.1 | async-start | bytes 589824 | tf_op jit(solution)/shard_map/all_to_all | solution.py:58
  36.3 86.8 %all-gather.3.cloned.1.call-start = ((), (), s32[]{:S(2)}) async-start(), calls=%async_computation.2 | async-start | bytes 2162688 | tf_op jit(solution)/shard_map/all_gather | solution.py:73
  123.1 9.1 %slice-start = ((s8[8388608]{0:T(1024)(128)(4,1)}), s8[4194304]{0:T(1024)(128)(4,1)S(1)}, s32[]{:S(2)}) async-start(s8[8388608]{0:T(1024)(128)(4,1)} %bitcast.54), calls=%async_computation.3 | async-start | bytes 8388608
  126.1 6.1 %slice-start.1 = ((s8[8388608]{0:T(1024)(128)(4,1)}), s8[4194304]{0:T(1024)(128)(4,1)S(1)}, s32[]{:S(2)}) async-start(s8[8388608]{0:T(1024)(128)(4,1)} %bitcast.54), calls=%async_computation.4 | async-start | bytes 8388608
Sparse Core Ops, SparseCore 0:
  50.0 72.9 all-gather.2
where the time goes:
time: 144 us; the launch traced here: 143 us
  waiting for transfers between devices  72 us (50%)
  local copies, waits for them, and re-layouts  22.5 us (16%)
  starting transfers between devices  16.4 us (11%)
  between operations  14.4 us (10%)
  matrix products  13.3 us (9%)
  other arithmetic  4.63 us (3%)
    all_gather x1, waiting for transfers between devices, body(): piece = lax.all_gather(own_field[None], 'sub', axis=0, tiled=True)  56.9 us
    unnamed x16, local copies, waits for them, and re-layouts  17 us
    all_to_all x1, waiting for transfers between devices, body(): lax.all_to_all(picked, 'sub', split_axis=1, concat_axis=0, tiled=True)  12.5 us
    all_to_all x1, starting transfers between devices, body(): lax.all_to_all(picked, 'sub', split_axis=1, concat_axis=0, tiled=True)  10.7 us
    dot_general x1, matrix products, body(): jnp.dot(masked, ancestor_blocks.reshape(LEVELS * BW, group_cols), preferr...  6.06 us
    all_to_all x1, starting transfers between devices, body(): lax.all_to_all(regrouped, 'vec', split_axis=0, concat_axis=2, tiled=True)  5.45 us
    dot_general x1, matrix products, body(): jnp.einsum('lc,cbk->lbk', select, piece, preferred_element_type=jnp.float32)  3 us
    dot_general x1, matrix products, body(): lax.dot_general(interior_modes, interior_coef, contract, preferred_elemen...  2.9 us
  transfers between devices with their start and end apart: 3, of which 3 were waited for; matrix products, arithmetic and copies ran while one was open for 13% of the time, Pallas kernels for 0%

commit v1 on v0

v1 whole, which is shorter than its diff:
```python
import jax
import jax.numpy as jnp
from jax import lax
from jax.experimental import pallas as pl
from jax.experimental.pallas import tpu as pltpu
from jax.sharding import PartitionSpec as P

BW = 256
SEPM = 128
LEVELS = 3
N_SUB = 32
N_Z = 8
N_VEC = 8
ROWS = 4
TILES_A = 20
TILES_I = 128
WIN = 9
SEPS = 1 + LEVELS
CAP = 1024
PHYS = 4096
NBLK = PHYS // BW
MESH = pl.DeviceIdType.MESH
BF16 = jnp.bfloat16
F32 = jnp.float32
NT = (((1,), (1,)), ((), ()))


def kernel(
    counts,
    ancestors,
    gates,
    coef_hbm,
    modes_hbm,
    sep_hbm,
    coupling_hbm,
    out,
    field,
    coef,
    modes,
    sep,
    coupling,
    send_a,
    recv_a,
    send_s,
    recv_s,
    send_w,
    recv_w,
    sep_coef,
    win_coef,
    above,
    total,
    weights,
    load_sem,
    send_a_sem,
    recv_a_sem,
    send_s_sem,
    recv_s_sem,
    send_w_sem,
    recv_w_sem,
):
    me = lax.axis_index("sub")
    mv = lax.axis_index("vec")
    barrier = pltpu.get_barrier_semaphore()

    def greet_vec(i, c):
        pl.semaphore_signal(
            barrier, inc=1, device_id={"vec": lax.rem(mv + i, N_VEC)}, device_id_type=MESH
        )
        return c

    def greet_sub(i, c):
        pl.semaphore_signal(
            barrier, inc=1, device_id={"sub": lax.rem(me + i, N_SUB)}, device_id_type=MESH
        )
        return c

    lax.fori_loop(1, N_VEC, greet_vec, 0)
    lax.fori_loop(1, N_SUB, greet_sub, 0)

    load_coef = pltpu.make_async_copy(coef_hbm, coef, load_sem.at[0])
    load_sep = pltpu.make_async_copy(sep_hbm, sep, load_sem.at[1])
    load_coupling = pltpu.make_async_copy(coupling_hbm, coupling, load_sem.at[2])
    load_modes = pltpu.make_async_copy(modes_hbm, modes, load_sem.at[3])
    load_coef.start()
    load_coef.wait()

    def split_rows(t, c):
        cols = pl.ds(pl.multiple_of(t * 128, 128), 128)
        for v in range(N_VEC):
            send_a[v, t] = coef[ROWS * v : ROWS * (v + 1), cols]
        return c

    lax.fori_loop(0, TILES_A, split_rows, 0)
    load_sep.start()
    load_coupling.start()
    load_modes.start()
    pl.semaphore_wait(barrier, N_VEC + N_SUB - 2)

    def copy_a(v):
        return pltpu.make_async_remote_copy(
            src_ref=send_a.at[v],
            dst_ref=recv_a.at[pl.ds(mv * TILES_A, TILES_A)],
            send_sem=send_a_sem.at[v],
            recv_sem=recv_a_sem.at[mv],
            device_id={"vec": v},
            device_id_type=MESH,
        )

    def own_a():
        return pltpu.make_async_copy(
            send_a.at[mv], recv_a.at[pl.ds(mv * TILES_A, TILES_A)], recv_a_sem.at[mv]
        )

    def start_a(i, c):
        copy_a(lax.rem(mv + i, N_VEC)).start()
        return c

    lax.fori_loop(1, N_VEC, start_a, 0)
    own_a().start()

    def wait_a(v, c):
        pltpu.make_async_copy(
            recv_a.at[pl.ds(v * TILES_A, TILES_A)],
            recv_a.at[pl.ds(v * TILES_A, TILES_A)],
            recv_a_sem.at[v],
        ).wait()
        return c

    lax.fori_loop(0, N_VEC, wait_a, 0)

    for s in range(N_SUB):
        send_s[s, 0] = recv_a[TILES_I + s]
        for l in range(LEVELS):
            send_s[s, 1 + l] = recv_a[TILES_I + ancestors[l, s]]

    def target(i):
        j = i // 4
        h = (j + 1) // 2
        dz = lax.rem(4 + h * (1 - 2 * lax.rem(j, 2)), N_Z)
        dx = lax.rem(i, 4)
        x = lax.rem(me // N_Z + dx, N_SUB // N_Z)
        z = lax.rem(lax.rem(me, N_Z) + dz, N_Z)
        return x * N_Z + z

    def remote(src, dst, ssem, rsem, s):
        return pltpu.make_async_remote_copy(
            src_ref=src.at[s],
            dst_ref=dst.at[me],
            send_sem=ssem.at[s],
            recv_sem=rsem.at[me],
            device_id={"sub": s},
            device_id_type=MESH,
        )

    def start_s(i, c):
        remote(send_s, recv_s, send_s_sem, recv_s_sem, target(i)).start()
        return c

    lax.fori_loop(0, N_SUB - 4, start_s, 0)
    lax.fori_loop(N_SUB - 3, N_SUB, start_s, 0)
    pltpu.make_async_copy(send_s.at[me], recv_s.at[me], recv_s_sem.at[me]).start()

    offset = jnp.int32(0)
    my_off = jnp.int32(0)
    for s in range(N_SUB):
        send_w[s] = recv_a[pl.ds(offset >> 7, WIN)]
        my_off = my_off + jnp.where(s < me, counts[s], 0)
        offset = offset + counts[s]

    def start_w(i, c):
        remote(send_w, recv_w, send_w_sem, recv_w_sem, target(i)).start()
        return c

    lax.fori_loop(0, N_SUB - 4, start_w, 0)
    lax.fori_loop(N_SUB - 3, N_SUB, start_w, 0)
    pltpu.make_async_copy(send_w.at[me], recv_w.at[me], recv_w_sem.at[me]).start()

    def gather_s(g, c):
        for q in range(4):
            s = g * 4 + q
            pltpu.make_async_copy(recv_s.at[s], recv_s.at[s], recv_s_sem.at[s]).wait()
            for t in range(SEPS):
                sep_coef[g, ROWS * q : ROWS * (q + 1), t * 128 : (t + 1) * 128] = recv_s[s, t]
        return c

    lax.fori_loop(0, N_SUB // 4, gather_s, 0)
    load_sep.wait()

    def field_of(index, t):
        block = sep_coef[:, :, t * 128 : (t + 1) * 128].reshape(128, 128)
        rows = sep[index]
        return lax.dot_general(rows, block, NT, preferred_element_type=F32).astype(BF16)

    field[...] = field_of(me, 0)
    for l in range(LEVELS):
        above[l * BW : (l + 1) * BW, :] = field_of(ancestors[l, me], 1 + l)
    load_coupling.wait()

    def couple(b, c):
        rows = pl.ds(pl.multiple_of(b * BW, BW), BW)
        acc = jnp.zeros((BW, 128), F32)
        for l in range(LEVELS):
            gate = gates[l, 0, b].astype(F32)
            acc = acc + gate * jnp.dot(
                coupling[rows, l * BW : (l + 1) * BW],
                above[l * BW : (l + 1) * BW, :],
                preferred_element_type=F32,
            )
        total[rows, :] = acc
        return c

    lax.fori_loop(0, NBLK, couple, 0)

    my_count = counts[me]
    shift = my_off & 127

    def gather_w(g, c):
        for q in range(4):
            s = g * 4 + q
            pltpu.make_async_copy(recv_w.at[s], recv_w.at[s], recv_w_sem.at[s]).wait()
            for t in range(WIN):
                win_coef[g, ROWS * q : ROWS * (q + 1), t * 128 : (t + 1) * 128] = recv_w[s, t]
        return c

    lax.fori_loop(0, N_SUB // 4, gather_w, 0)
    row = lax.broadcasted_iota(jnp.int32, (128, 256), 0)
    col = lax.broadcasted_iota(jnp.int32, (128, 256), 1)
    for t in range(CAP // 128):
        pick = jnp.where((col == row + shift) & (row + t * 128 < my_count), 1.0, 0.0).astype(BF16)
        pair = win_coef[:, :, t * 128 : (t + 2) * 128].reshape(128, 256)
        weights[t * 128 : (t + 1) * 128, :] = lax.dot_general(
            pick, pair, NT, preferred_element_type=F32
        ).astype(BF16)
    load_modes.wait()

    def finish(b, c):
        rows = pl.ds(pl.multiple_of(b * 512, 512), 512)
        part = jnp.dot(modes[rows, :], weights[...], preferred_element_type=F32)
        out[rows, :] = (total[rows, :] + part).astype(BF16)
        return c

    lax.fori_loop(0, PHYS // 512, finish, 0)

    def drain_a(i, c):
        copy_a(lax.rem(mv + i, N_VEC)).wait_send()
        return c

    def drain_b(i, c):
        s = lax.rem(me + i, N_SUB)
        remote(send_s, recv_s, send_s_sem, recv_s_sem, s).wait_send()
        remote(send_w, recv_w, send_w_sem, recv_w_sem, s).wait_send()
        return c

    lax.fori_loop(1, N_VEC, drain_a, 0)
    lax.fori_loop(1, N_SUB, drain_b, 0)


def body(coefficients, row_counts, ancestors, interior_modes, separator_modes, coupling, pattern):
    smem = pl.BlockSpec(memory_space=pltpu.SMEM)
    hbm = pl.BlockSpec(memory_space=pl.ANY)
    vmem = pl.BlockSpec(memory_space=pltpu.VMEM)
    dma = pltpu.SemaphoreType.DMA
    return pl.pallas_call(
        kernel,
        out_shape=(
            jax.ShapeDtypeStruct((PHYS, 128), BF16),
            jax.ShapeDtypeStruct((BW, 128), BF16),
        ),
        in_specs=[smem, smem, smem, hbm, hbm, hbm, hbm],
        out_specs=(vmem, vmem),
        scratch_shapes=[
            pltpu.VMEM((ROWS * N_VEC, TILES_A * 128), BF16),
            pltpu.VMEM((PHYS, CAP), BF16),
            pltpu.VMEM((N_SUB, BW, SEPM), BF16),
            pltpu.VMEM((PHYS, LEVELS * BW), BF16),
            pltpu.VMEM((N_VEC, TILES_A, ROWS, 128), BF16),
            pltpu.VMEM((N_VEC * TILES_A, ROWS, 128), BF16),
            pltpu.VMEM((N_SUB, SEPS, ROWS, 128), BF16),
            pltpu.VMEM((N_SUB, SEPS, ROWS, 128), BF16),
            pltpu.VMEM((N_SUB, WIN, ROWS, 128), BF16),
            pltpu.VMEM((N_SUB, WIN, ROWS, 128), BF16),
            pltpu.VMEM((N_SUB // 4, 4 * ROWS, SEPS * 128), BF16),
            pltpu.VMEM((N_SUB // 4, 4 * ROWS, WIN * 128), BF16),
            pltpu.VMEM((LEVELS * BW, 128), BF16),
            pltpu.VMEM((PHYS, 128), F32),
            pltpu.VMEM((CAP, 128), BF16),
            dma((4,)),
            dma((N_VEC,)),
            dma((N_VEC,)),
            dma((N_SUB,)),
            dma((N_SUB,)),
            dma((N_SUB,)),
            dma((N_SUB,)),
        ],
        compiler_params=pltpu.CompilerParams(
            collective_id=0, has_side_effects=True, vmem_limit_bytes=60 * 1024 * 1024
        ),
        name="recover",
    )(
        row_counts,
        ancestors.T,
        jnp.transpose(pattern, (2, 0, 1)),
        coefficients,
        interior_modes,
        separator_modes.reshape(N_SUB, BW, SEPM),
        coupling,
    )


def solution(mesh):
    placed = (P("sub", "vec"), P(), P(), P("sub", None), P(), P("sub", None), P("sub", None, None))
    return jax.shard_map(
        body,
        mesh=mesh,
        in_specs=placed,
        out_specs=(P("sub", "vec"), P("sub", "vec")),
        check_vma=False,
    )
```

time: 144 us -> 39.9 us (0.28)
  the two profiles are of different devices: /device:TPU:8 before, /device:TPU:1 now
where the time goes in v1:
time: 39.9 us; the launch traced here: 39.7 us
  Pallas kernels  35.3 us (88%)
  local copies, waits for them, and re-layouts  3.73 us (9%)
  between operations  0.64 us (2%)
    pallas_call x1, Pallas kernels, body(): pl.pallas_call(kernel, out_shape=(jax.ShapeDtypeStruct((PHYS, 128), BF16)...  35.3 us
    unnamed x2, local copies, waits for them, and re-layouts  3.73 us

profile of v1, /device:TPU:1, one launch (start us, length us, event | category | flops | bytes accessed | tf_op | source)
XLA Modules:
  0.0 39.7 jit_solution(16511543690749470013)
XLA Ops:
  0.6 35.3 %recover.1 = (bf16[4096,128]{1,0:T(8,128)(2,1)}, bf16[256,128]{1,0:T(8,128)(2,1)}) custom-call(s32[32]{0:T(128)} %counts.1, s32[3,32]{1,0:T(4,128)} %bitcast.4, s32[3,1,16]{2,1,0:T(1,128)} %bitcast.5, bf16[32,2560]{1,0:T(8,128)(2,1)} %coef_hbm.1, bf16[4096,1024]{1,0:T(8,128)(2,1)} %modes_hbm.1, bf16[32,256,128]{2,1,0:T(8,128)(2,1)} %bitcast.3, ...), custom_call_target="tpu_custom_call" | custom-call | tf_op jit(solution)/shard_map/recover/pallas_call | solution.py:263
  35.9 2.3 %copy.11 = bf16[4096,128]{1,0:T(8,128)(2,1)} copy(bf16[4096,128]{1,0:T(8,128)(2,1)} %get-tuple-element.4) | data formatting | bytes 2097152
  38.2 1.5 %copy.12 = bf16[256,128]{1,0:T(8,128)(2,1)} copy(bf16[256,128]{1,0:T(8,128)(2,1)} %get-tuple-element.5) | data formatting | bytes 131072

commit v2 on v1

v2 whole, which is shorter than its diff:
```python
import jax
import jax.numpy as jnp
from jax import lax
from jax.experimental import pallas as pl
from jax.experimental.pallas import tpu as pltpu
from jax.sharding import PartitionSpec as P

BW = 256
SEPM = 128
LEVELS = 3
N_SUB = 32
N_X = 4
N_Z = 8
N_VEC = 8
ROWS = 4
TILES_A = 20
TILES_I = 128
SEPS = 1 + LEVELS
WIN = 9
GROUPS = ((0, SEPS), (SEPS, 5), (SEPS + 5, 2), (SEPS + 7, 2))
CHUNKS = ((0, 4), (4, 2), (6, 2))
SLOT = SEPS + WIN
CAP = 1024
PHYS = 4096
NBLK = PHYS // BW
MESH = pl.DeviceIdType.MESH
BF16 = jnp.bfloat16
F32 = jnp.float32
NT = (((1,), (1,)), ((), ()))


def kernel(
    counts_hbm,
    ancestors_hbm,
    gates_hbm,
    coef_hbm,
    modes_hbm,
    sep_hbm,
    coupling_hbm,
    out,
    field,
    counts,
    ancestors,
    gates,
    coef,
    modes,
    sep,
    coupling,
    send_a,
    recv_a,
    send_b,
    recv_b,
    lanes,
    above,
    total,
    weights,
    load_sem,
    send_a_sem,
    recv_a_sem,
    send_b_sem,
    recv_b_sem,
    relay_sem,
):
    me = lax.axis_index("sub")
    mv = lax.axis_index("vec")
    mx = lax.div(me, N_Z)
    mz = lax.rem(me, N_Z)
    z_up = mx * N_Z + lax.rem(mz + 1, N_Z)
    z_down = mx * N_Z + lax.rem(mz + N_Z - 1, N_Z)
    x_up = lax.rem(mx + 1, N_X) * N_Z + mz
    x_down = lax.rem(mx + N_X - 1, N_X) * N_Z + mz

    def load(src, dst, i):
        return pltpu.make_async_copy(src, dst, load_sem.at[i])

    load_coef = load(coef_hbm, coef, 0)
    load_sep = load(sep_hbm, sep, 1)
    load_coupling = load(coupling_hbm, coupling, 2)
    load_modes = load(modes_hbm, modes, 3)
    load_counts = load(counts_hbm, counts, 4)
    load_ancestors = load(ancestors_hbm, ancestors, 5)
    load_gates = load(gates_hbm, gates, 6)

    barrier = pltpu.get_barrier_semaphore()
    for i in range(1, N_VEC):
        pl.semaphore_signal(
            barrier, inc=1, device_id={"vec": lax.rem(mv + i, N_VEC)}, device_id_type=MESH
        )
    for s in (z_up, z_down, x_up, x_down):
        pl.semaphore_signal(barrier, inc=1, device_id={"sub": s}, device_id_type=MESH)
    load_coef.start()
    load_counts.start()
    load_ancestors.start()
    load_gates.start()
    load_sep.start()
    load_coupling.start()
    load_modes.start()
    load_coef.wait()

    def split_rows(t, c):
        cols = pl.ds(pl.multiple_of(t * 128, 128), 128)
        for v in range(N_VEC):
            send_a[v, t] = coef[ROWS * v : ROWS * (v + 1), cols]
        return c

    lax.fori_loop(0, TILES_A, split_rows, 0)
    pl.semaphore_wait(barrier, N_VEC - 1 + 4)

    def copy_a(v):
        return pltpu.make_async_remote_copy(
            src_ref=send_a.at[v],
            dst_ref=recv_a.at[pl.ds(mv * TILES_A, TILES_A)],
            send_sem=send_a_sem.at[v],
            recv_sem=recv_a_sem.at[mv],
            device_id={"vec": v},
            device_id_type=MESH,
        )

    def start_a(i, c):
        copy_a(lax.rem(mv + i, N_VEC)).start()
        return c

    lax.fori_loop(1, N_VEC, start_a, 0)
    pltpu.make_async_copy(
        send_a.at[mv], recv_a.at[pl.ds(mv * TILES_A, TILES_A)], recv_a_sem.at[mv]
    ).start()

    for r in range(5):
        up, down = (z_up, z_down) if r < 3 else (x_up, x_down)
        pl.semaphore_signal(
            relay_sem.at[2 * r], inc=1, device_id={"sub": up}, device_id_type=MESH
        )
        pl.semaphore_signal(
            relay_sem.at[2 * r + 1], inc=1, device_id={"sub": down}, device_id_type=MESH
        )
        pl.semaphore_wait(relay_sem.at[2 * r], 1)
        pl.semaphore_wait(relay_sem.at[2 * r + 1], 1)

    load_counts.wait()
    load_ancestors.wait()
    load_gates.wait()

    def wait_a(v, c):
        block = recv_a.at[pl.ds(v * TILES_A, TILES_A)]
        pltpu.make_async_copy(block, block, recv_a_sem.at[v]).wait()
        return c

    lax.fori_loop(0, N_VEC, wait_a, 0)

    def remote(g, s):
        start, size = GROUPS[g]
        return pltpu.make_async_remote_copy(
            src_ref=send_b.at[s, pl.ds(start, size)],
            dst_ref=recv_b.at[me, pl.ds(start, size)],
            send_sem=send_b_sem.at[g, s],
            recv_sem=recv_b_sem.at[g, me],
            device_id={"sub": s},
            device_id_type=MESH,
        )

    def send_group(g):
        def row(j, xs):
            h = lax.div(j + 1, 2)
            dz = 4 + h * (1 - 2 * lax.rem(j, 2))
            z = lax.rem(mz + dz, N_Z)
            for dx in xs:
                remote(g, lax.rem(mx + dx, N_X) * N_Z + z).start()

        def step(j, c):
            row(j, range(N_X))
            return c

        lax.fori_loop(0, N_Z - 1, step, 0)
        row(N_Z - 1, range(1, N_X))
        start, size = GROUPS[g]
        pltpu.make_async_copy(
            send_b.at[me, pl.ds(start, size)],
            recv_b.at[me, pl.ds(start, size)],
            recv_b_sem.at[g, me],
        ).start()

    for s in range(N_SUB):
        send_b[s, 0] = recv_a[TILES_I + s]
        for l in range(LEVELS):
            send_b[s, 1 + l] = recv_a[TILES_I + ancestors[l, s]]
    send_group(0)
    offset = jnp.int32(0)
    my_off = jnp.int32(0)
    for s in range(N_SUB):
        send_b[s, SEPS:] = recv_a[pl.ds(offset >> 7, WIN)]
        my_off = my_off + jnp.where(s < me, counts[s], 0)
        offset = offset + counts[s]
    for g in range(1, len(GROUPS)):
        send_group(g)
    my_count = counts[me]
    shift = my_off & 127

    def drain_a(i, c):
        copy_a(lax.rem(mv + i, N_VEC)).wait_send()
        return c

    def drain(g):
        def step(i, c):
            remote(g, lax.rem(me + i, N_SUB)).wait_send()
            return c

        lax.fori_loop(1, N_SUB, step, 0)

    def gather(g):
        start, size = GROUPS[g]

        def step(k, c):
            for q in range(4):
                s = k * 4 + q
                block = recv_b.at[s, pl.ds(start, size)]
                pltpu.make_async_copy(block, block, recv_b_sem.at[g, s]).wait()
                for t in range(start, start + size):
                    lanes[k, ROWS * q : ROWS * (q + 1), t * 128 : (t + 1) * 128] = recv_b[s, t]
            return c

        lax.fori_loop(0, N_SUB // 4, step, 0)

    lax.fori_loop(1, N_VEC, drain_a, 0)
    load_coupling.wait()

    def mask(b, c):
        rows = pl.ds(pl.multiple_of(b * BW, BW), BW)
        for l in range(LEVELS):
            cols = slice(l * BW, (l + 1) * BW)
            gate = gates[l, 0, b].astype(F32).astype(BF16)
            coupling[rows, cols] = coupling[rows, cols] * gate
        return c

    lax.fori_loop(0, NBLK, mask, 0)
    load_sep.wait()
    load_modes.wait()
    gather(0)

    def field_of(index, t):
        block = lanes[:, :, t * 128 : (t + 1) * 128].reshape(128, 128)
        return lax.dot_general(sep[index], block, NT, preferred_element_type=F32).astype(BF16)

    field[...] = field_of(me, 0)
    for l in range(LEVELS):
        above[l * BW : (l + 1) * BW, :] = field_of(ancestors[l, me], 1 + l)

    def couple(b, c):
        rows = pl.ds(pl.multiple_of(b * 512, 512), 512)
        total[rows, :] = jnp.dot(coupling[rows, :], above[...], preferred_element_type=F32)
        return c

    lax.fori_loop(0, PHYS // 512, couple, 0)
    row = lax.broadcasted_iota(jnp.int32, (128, 256), 0)
    col = lax.broadcasted_iota(jnp.int32, (128, 256), 1)

    def interior(g):
        first, count = CHUNKS[g]
        gather(g + 1)
        for t in range(first, first + count):
            pick = jnp.where((col == row + shift) & (row + t * 128 < my_count), 1.0, 0.0)
            pair = lanes[:, :, (SEPS + t) * 128 : (SEPS + t + 2) * 128].reshape(128, 256)
            weights[t * 128 : (t + 1) * 128, :] = lax.dot_general(
                pick.astype(BF16), pair, NT, preferred_element_type=F32
            ).astype(BF16)
        cols = slice(first * 128, (first + count) * 128)

        def step(b, c):
            rows = pl.ds(pl.multiple_of(b * 512, 512), 512)
            part = total[rows, :] + jnp.dot(
                modes[rows, cols], weights[cols, :], preferred_element_type=F32
            )
            if g < len(CHUNKS) - 1:
                total[rows, :] = part
            else:
                out[rows, :] = part.astype(BF16)
            return c

        lax.fori_loop(0, PHYS // 512, step, 0)

    interior(0)
    interior(1)
    for g in range(len(GROUPS) - 1):
        drain(g)
    interior(2)
    drain(len(GROUPS) - 1)


def body(coefficients, row_counts, ancestors, interior_modes, separator_modes, coupling, pattern):
    hbm = pl.BlockSpec(memory_space=pl.ANY)
    vmem = pl.BlockSpec(memory_space=pltpu.VMEM)
    dma = pltpu.SemaphoreType.DMA
    return pl.pallas_call(
        kernel,
        out_shape=(pltpu.VMEM((PHYS, 128), BF16), pltpu.VMEM((BW, 128), BF16)),
        in_specs=[hbm] * 7,
        out_specs=(vmem, vmem),
        scratch_shapes=[
            pltpu.SMEM((N_SUB,), jnp.int32),
            pltpu.SMEM((LEVELS, N_SUB), jnp.int32),
            pltpu.SMEM((LEVELS, 1, NBLK), jnp.int32),
            pltpu.VMEM((ROWS * N_VEC, TILES_A * 128), BF16),
            pltpu.VMEM((PHYS, CAP), BF16),
            pltpu.VMEM((N_SUB, BW, SEPM), BF16),
            pltpu.VMEM((PHYS, LEVELS * BW), BF16),
            pltpu.VMEM((N_VEC, TILES_A, ROWS, 128), BF16),
            pltpu.VMEM((N_VEC * TILES_A, ROWS, 128), BF16),
            pltpu.VMEM((N_SUB, SLOT, ROWS, 128), BF16),
            pltpu.VMEM((N_SUB, SLOT, ROWS, 128), BF16),
            pltpu.VMEM((N_SUB // 4, 4 * ROWS, SLOT * 128), BF16),
            pltpu.VMEM((LEVELS * BW, 128), BF16),
            pltpu.VMEM((PHYS, 128), F32),
            pltpu.VMEM((CAP, 128), BF16),
            dma((7,)),
            dma((N_VEC,)),
            dma((N_VEC,)),
            dma((len(GROUPS), N_SUB)),
            dma((len(GROUPS), N_SUB)),
            pltpu.SemaphoreType.REGULAR((10,)),
        ],
        compiler_params=pltpu.CompilerParams(
            collective_id=0, has_side_effects=True, vmem_limit_bytes=60 * 1024 * 1024
        ),
        name="recover",
    )(
        row_counts,
        ancestors.T,
        jnp.transpose(pattern, (2, 0, 1)),
        coefficients,
        interior_modes,
        separator_modes.reshape(N_SUB, BW, SEPM),
        coupling,
    )


def solution(mesh):
    placed = (P("sub", "vec"), P(), P(), P("sub", None), P(), P("sub", None), P("sub", None, None))
    return jax.shard_map(
        body,
        mesh=mesh,
        in_specs=placed,
        out_specs=(P("sub", "vec"), P("sub", "vec")),
        check_vma=False,
    )
```

time: 39.9 us -> 39.8 us (level)
  the two profiles are of different devices: /device:TPU:1 before, /device:TPU:2 now
where the time goes in v2:
time: 39.8 us; the launch traced here: 39.7 us
  Pallas kernels  37.5 us (94%)
  local copies, waits for them, and re-layouts  1.6 us (4%)
  between operations  0.64 us (2%)
    pallas_call x1, Pallas kernels, body(): pl.pallas_call(kernel, out_shape=(pltpu.VMEM((PHYS, 128), BF16), pltpu.VM...  37.5 us
    unnamed x2, local copies, waits for them, and re-layouts  1.6 us

profile of v2, /device:TPU:2, one launch (start us, length us, event | category | flops | bytes accessed | tf_op | source)
XLA Modules:
  0.0 39.7 jit_solution(1680530989552650143)
XLA Ops:
  0.6 37.5 %recover.1 = (bf16[4096,128]{1,0:T(8,128)(2,1)S(1)}, bf16[256,128]{1,0:T(8,128)(2,1)S(1)}) custom-call(s32[32]{0:T(128)} %counts_hbm.1, s32[3,32]{1,0:T(4,128)} %bitcast.4, s32[3,1,16]{2,1,0:T(1,128)} %bitcast.5, bf16[32,2560]{1,0:T(8,128)(2,1)} %coef_hbm.1, bf16[4096,1024]{1,0:T(8,128)(2,1)} %modes_hbm.1, bf16[32,256,128]{2,1,0:T(8,128)(2,1)} %bitcast.3, ...), custom_call_target="tpu_custom_call" | custom-call | tf_op jit(solution)/shard_map/recover/pallas_call | solution.py:292
  38.1 1.0 %copy.11 = bf16[4096,128]{1,0:T(8,128)(2,1)} copy(bf16[4096,128]{1,0:T(8,128)(2,1)S(1)} %get-tuple-element.2) | data formatting | bytes 2097152
  39.1 0.6 %copy.12 = bf16[256,128]{1,0:T(8,128)(2,1)} copy(bf16[256,128]{1,0:T(8,128)(2,1)S(1)} %get-tuple-element.3) | data formatting | bytes 131072

commit v3 on v2

v3 whole, which is shorter than its diff:
```python
import jax
import jax.numpy as jnp
from jax import lax
from jax.experimental import pallas as pl
from jax.experimental.pallas import tpu as pltpu
from jax.sharding import PartitionSpec as P

BW = 256
SEPM = 128
LEVELS = 3
N_SUB = 32
N_X = 4
N_Z = 8
N_VEC = 8
ROWS = 4
TILES_A = 20
TILES_I = 128
SEPS = 1 + LEVELS
WIN = 9
GROUPS = ((0, WIN, 0, 8),)
CAP = 1024
PHYS = 4096
NBLK = PHYS // BW
MESH = pl.DeviceIdType.MESH
BF16 = jnp.bfloat16
F32 = jnp.float32
NT = (((1,), (1,)), ((), ()))


def kernel(
    counts_hbm,
    ancestors_hbm,
    gates_hbm,
    coef_hbm,
    modes_hbm,
    sep_hbm,
    coupling_hbm,
    out,
    field,
    counts,
    ancestors,
    gates,
    coef,
    modes,
    sep,
    coupling,
    send_a,
    recv_i,
    recv_s,
    lanes,
    above,
    total,
    weights,
    load_sem,
    send_a_sem,
    recv_a_sem,
    send_b_sem,
    recv_b_sem,
    relay_sem,
    *slots,
):
    send_b = slots[: len(slots) // 2]
    recv_b = slots[len(slots) // 2 :]
    me = lax.axis_index("sub")
    mv = lax.axis_index("vec")
    mx = lax.div(me, N_Z)
    mz = lax.rem(me, N_Z)

    def along_z(d):
        return mx * N_Z + lax.rem(mz + N_Z + d, N_Z)

    def along_x(d):
        return lax.rem(mx + N_X + d, N_X) * N_Z + mz

    def load(src, dst, i):
        return pltpu.make_async_copy(src, dst, load_sem.at[i])

    load_coef = load(coef_hbm, coef, 0)
    load_sep = load(sep_hbm, sep, 1)
    load_coupling = load(coupling_hbm, coupling, 2)
    load_modes = load(modes_hbm, modes, 3)
    load_counts = load(counts_hbm, counts, 4)
    load_ancestors = load(ancestors_hbm, ancestors, 5)
    load_gates = load(gates_hbm, gates, 6)

    barrier = pltpu.get_barrier_semaphore()
    for i in range(1, N_VEC):
        pl.semaphore_signal(
            barrier, inc=1, device_id={"vec": lax.rem(mv + i, N_VEC)}, device_id_type=MESH
        )
    near = [along_z(d) for d in (1, -1, 2, -2)] + [along_x(d) for d in (1, -1, 2)]
    for s in near:
        pl.semaphore_signal(barrier, inc=1, device_id={"sub": s}, device_id_type=MESH)
    load_coef.start()
    load_counts.start()
    load_ancestors.start()
    load_gates.start()
    load_sep.start()
    load_coupling.start()
    load_modes.start()
    load_coef.wait()

    def split_rows(t, c):
        cols = pl.ds(pl.multiple_of(t * 128, 128), 128)
        for v in range(N_VEC):
            send_a[v, t] = coef[ROWS * v : ROWS * (v + 1), cols]
        return c

    lax.fori_loop(0, TILES_A, split_rows, 0)
    recv_i[TILES_I:] = jnp.zeros((WIN - 1, ROWS, 128), BF16)
    pl.semaphore_wait(barrier, N_VEC - 1 + len(near))

    def tell(i, s):
        pl.semaphore_signal(relay_sem.at[i], inc=1, device_id={"sub": s}, device_id_type=MESH)

    tell(0, along_z(2))
    tell(1, along_z(-2))

    def send_rows(group, start, size):
        def own(v):
            return send_a.at[v, pl.ds(start, size)]

        there = (recv_s, recv_i)[group].at[
            pl.ds(mv * TILES_A + start - (0 if group else TILES_I), size)
        ]

        def step(i, c):
            v = lax.rem(mv + i, N_VEC)
            pltpu.make_async_remote_copy(
                src_ref=own(v),
                dst_ref=there,
                send_sem=send_a_sem.at[0],
                recv_sem=recv_a_sem.at[group],
                device_id={"vec": v},
                device_id_type=MESH,
            ).start()
            return c

        lax.fori_loop(1, N_VEC, step, 0)
        pltpu.make_async_copy(own(mv), there, recv_a_sem.at[group]).start()

    split = TILES_I // TILES_A
    cut = TILES_I - split * TILES_A

    @pl.when(mv < split)
    def _():
        send_rows(1, 0, TILES_A)

    @pl.when(mv == split)
    def _():
        send_rows(0, cut, TILES_A - cut)
        send_rows(1, 0, cut)

    @pl.when(mv > split)
    def _():
        send_rows(0, 0, TILES_A)

    def settle(ref, sem):
        pltpu.make_async_copy(ref, ref, sem).wait()

    load_counts.wait()
    load_ancestors.wait()
    load_gates.wait()
    pl.semaphore_wait(relay_sem.at[0], 1)
    pl.semaphore_wait(relay_sem.at[1], 1)
    tell(2, along_x(1))
    tell(3, along_x(-1))
    tell(4, along_x(2))
    pl.semaphore_wait(relay_sem.at[2], 1)
    pl.semaphore_wait(relay_sem.at[3], 1)
    pl.semaphore_wait(relay_sem.at[4], 1)

    def send_group(g):
        def row(j, xs):
            h = lax.div(j + 1, 2)
            dz = 4 + h * (1 - 2 * lax.rem(j, 2))
            z = lax.rem(mz + dz, N_Z)
            for dx in xs:
                s = lax.rem(mx + dx, N_X) * N_Z + z
                pltpu.make_async_remote_copy(
                    src_ref=send_b[g].at[s],
                    dst_ref=recv_b[g].at[me],
                    send_sem=send_b_sem.at[g],
                    recv_sem=recv_b_sem.at[g],
                    device_id={"sub": s},
                    device_id_type=MESH,
                ).start()

        def step(j, c):
            row(j, range(N_X))
            return c

        lax.fori_loop(0, N_Z - 1, step, 0)
        row(N_Z - 1, range(1, N_X))
        pltpu.make_async_copy(send_b[g].at[me], recv_b[g].at[me], recv_b_sem.at[g]).start()

    settle(recv_s, recv_a_sem.at[0])
    for s in range(N_SUB):
        send_b[0][s, 0] = recv_s[s]
        for l in range(LEVELS):
            send_b[0][s, 1 + l] = recv_s[ancestors[l, s]]
    send_group(0)
    settle(recv_i.at[pl.ds(0, TILES_I)], recv_a_sem.at[1])
    offset = jnp.int32(0)
    my_off = jnp.int32(0)
    for s in range(N_SUB):
        for g, (start, size, _, _) in enumerate(GROUPS):
            send_b[1 + g][s] = recv_i[pl.ds((offset >> 7) + start, size)]
        my_off = my_off + jnp.where(s < me, counts[s], 0)
        offset = offset + counts[s]
    for g in range(len(GROUPS)):
        send_group(1 + g)
    my_count = counts[me]
    shift = my_off & 127

    def gather(g, start, size):
        settle(recv_b[g], recv_b_sem.at[g])

        def step(k, c):
            for q in range(4):
                for t in range(size):
                    cols = slice((start + t) * 128, (start + t + 1) * 128)
                    lanes[k, ROWS * q : ROWS * (q + 1), cols] = recv_b[g][k * 4 + q, t]
            return c

        lax.fori_loop(0, N_SUB // 4, step, 0)

    load_coupling.wait()

    def mask(b, c):
        rows = pl.ds(pl.multiple_of(b * BW, BW), BW)
        for l in range(LEVELS):
            cols = slice(l * BW, (l + 1) * BW)
            gate = gates[l, 0, b].astype(F32).astype(BF16)
            coupling[rows, cols] = coupling[rows, cols] * gate
        return c

    lax.fori_loop(0, NBLK, mask, 0)
    load_sep.wait()
    load_modes.wait()
    settle(send_a.at[pl.ds(0, N_VEC - 1)], send_a_sem.at[0])
    gather(0, 0, SEPS)

    def field_of(index, t):
        block = lanes[:, :, t * 128 : (t + 1) * 128].reshape(128, 128)
        return lax.dot_general(sep[index], block, NT, preferred_element_type=F32).astype(BF16)

    field[...] = field_of(me, 0)
    for l in range(LEVELS):
        above[l * BW : (l + 1) * BW, :] = field_of(ancestors[l, me], 1 + l)
    total[...] = jnp.dot(coupling[...], above[...], preferred_element_type=F32)
    row = lax.broadcasted_iota(jnp.int32, (128, 256), 0)
    col = lax.broadcasted_iota(jnp.int32, (128, 256), 1)
    for g, (start, size, first, last) in enumerate(GROUPS):
        gather(1 + g, SEPS + start, size)
        for t in range(first, last):
            pick = jnp.where((col == row + shift) & (row + t * 128 < my_count), 1.0, 0.0)
            pair = lanes[:, :, (SEPS + t) * 128 : (SEPS + t + 2) * 128].reshape(128, 256)
            weights[t * 128 : (t + 1) * 128, :] = lax.dot_general(
                pick.astype(BF16), pair, NT, preferred_element_type=F32
            ).astype(BF16)
        if g == len(GROUPS) - 1:
            for r in range(1 + len(GROUPS)):
                settle(send_b[r].at[pl.ds(0, N_SUB - 1)], send_b_sem.at[r])
        cols = slice(first * 128, last * 128)
        part = total[...] + jnp.dot(
            modes[:, cols], weights[cols, :], preferred_element_type=F32
        )
        if g < len(GROUPS) - 1:
            total[...] = part
        else:
            out[...] = part.astype(BF16)


def store(interior, field, interior_out, field_out, sem):
    copies = (
        pltpu.make_async_copy(interior, interior_out, sem.at[0]),
        pltpu.make_async_copy(field, field_out, sem.at[1]),
    )
    for copy in copies:
        copy.start()
    for copy in copies:
        copy.wait()


def body(coefficients, row_counts, ancestors, interior_modes, separator_modes, coupling, pattern):
    hbm = pl.BlockSpec(memory_space=pl.ANY)
    vmem = pl.BlockSpec(memory_space=pltpu.VMEM)
    dma = pltpu.SemaphoreType.DMA
    sizes = [SEPS] + [size for _, size, _, _ in GROUPS]
    slots = [pltpu.VMEM((N_SUB, size, ROWS, 128), BF16) for size in sizes]
    results = pl.pallas_call(
        kernel,
        out_shape=(pltpu.VMEM((PHYS, 128), BF16), pltpu.VMEM((BW, 128), BF16)),
        in_specs=[hbm] * 7,
        out_specs=(vmem, vmem),
        scratch_shapes=[
            pltpu.SMEM((N_SUB,), jnp.int32),
            pltpu.SMEM((LEVELS, N_SUB), jnp.int32),
            pltpu.SMEM((LEVELS, 1, NBLK), jnp.int32),
            pltpu.VMEM((ROWS * N_VEC, TILES_A * 128), BF16),
            pltpu.VMEM((PHYS, CAP), BF16),
            pltpu.VMEM((N_SUB, BW, SEPM), BF16),
            pltpu.VMEM((PHYS, LEVELS * BW), BF16),
            pltpu.VMEM((N_VEC, TILES_A, ROWS, 128), BF16),
            pltpu.VMEM((TILES_I + WIN - 1, ROWS, 128), BF16),
            pltpu.VMEM((N_SUB, ROWS, 128), BF16),
            pltpu.VMEM((N_SUB // 4, 4 * ROWS, (SEPS + WIN) * 128), BF16),
            pltpu.VMEM((LEVELS * BW, 128), BF16),
            pltpu.VMEM((PHYS, 128), F32),
            pltpu.VMEM((CAP, 128), BF16),
            dma((7,)),
            dma((1,)),
            dma((2,)),
            dma((len(sizes),)),
            dma((len(sizes),)),
            pltpu.SemaphoreType.REGULAR((5,)),
            *slots,
            *slots,
        ],
        compiler_params=pltpu.CompilerParams(
            collective_id=0, has_side_effects=True, vmem_limit_bytes=60 * 1024 * 1024
        ),
        name="recover",
    )(
        row_counts,
        ancestors.T,
        jnp.transpose(pattern, (2, 0, 1)),
        coefficients,
        interior_modes,
        separator_modes.reshape(N_SUB, BW, SEPM),
        coupling,
    )
    return pl.pallas_call(
        store,
        out_shape=tuple(jax.ShapeDtypeStruct((rows, 128), BF16) for rows in (PHYS, BW)),
        in_specs=[vmem] * 2,
        out_specs=(hbm, hbm),
        scratch_shapes=[dma((2,))],
        compiler_params=pltpu.CompilerParams(vmem_limit_bytes=8 * 1024 * 1024),
        name="store",
    )(*[pltpu.with_memory_space_constraint(x, pltpu.VMEM) for x in results])


def solution(mesh):
    placed = (P("sub", "vec"), P(), P(), P("sub", None), P(), P("sub", None), P("sub", None, None))
    return jax.shard_map(
        body,
        mesh=mesh,
        in_specs=placed,
        out_specs=(P("sub", "vec"), P("sub", "vec")),
        check_vma=False,
    )
```

time: 39.8 us -> 32.1 us (0.81)
  the two profiles are of different devices: /device:TPU:2 before, /device:TPU:1 now
where the time goes in v3:
time: 32.1 us; the launch traced here: 32 us
  Pallas kernels  31.4 us (98%)
  between operations  0.64 us (2%)
    pallas_call x1, Pallas kernels, body(): pl.pallas_call(kernel, out_shape=(pltpu.VMEM((PHYS, 128), BF16), pltpu.VM...  30.4 us
    pallas_call x1, Pallas kernels, body(): pl.pallas_call(store, out_shape=tuple((jax.ShapeDtypeStruct((rows, 128),...  0.99 us

profile of v3, /device:TPU:1, one launch (start us, length us, event | category | flops | bytes accessed | tf_op | source)
XLA Modules:
  0.0 32.0 jit_solution(16479077943094037338)
XLA Ops:
  0.6 30.4 %recover.1 = (bf16[4096,128]{1,0:T(8,128)(2,1)S(1)}, bf16[256,128]{1,0:T(8,128)(2,1)S(1)}) custom-call(s32[32]{0:T(128)} %counts_hbm.1, s32[3,32]{1,0:T(4,128)} %bitcast.4, s32[3,1,16]{2,1,0:T(1,128)} %bitcast.5, bf16[32,2560]{1,0:T(8,128)(2,1)} %coef_hbm.1, bf16[4096,1024]{1,0:T(8,128)(2,1)} %modes_hbm.1, bf16[32,256,128]{2,1,0:T(8,128)(2,1)} %bitcast.3, ...), custom_call_target="tpu_custom_call" | custom-call | tf_op jit(solution)/shard_map/recover/pallas_call | solution.py:292
  31.0 1.0 %store.1 = (bf16[4096,128]{1,0:T(8,128)(2,1)}, bf16[256,128]{1,0:T(8,128)(2,1)}) custom-call(bf16[4096,128]{1,0:T(8,128)(2,1)S(1)} %get-tuple-element.4.interior, bf16[256,128]{1,0:T(8,128)(2,1)S(1)} %get-tuple-element.5.field), custom_call_target="tpu_custom_call" | custom-call | tf_op jit(solution)/shard_map/store/pallas_call | solution.py:334

commit v4 on v3

--- a/solution.py
+++ b/solution.py
@@ -17,10 +17,11 @@
 TILES_I = 128
 SEPS = 1 + LEVELS
 WIN = 9
-GROUPS = ((0, WIN, 0, 8),)
+GROUPS = ((0, 5, 0, 4), (5, 4, 4, 8))
 CAP = 1024
 PHYS = 4096
 NBLK = PHYS // BW
+STEP = 2048
 MESH = pl.DeviceIdType.MESH
 BF16 = jnp.bfloat16
 F32 = jnp.float32
@@ -248,7 +249,13 @@
     field[...] = field_of(me, 0)
     for l in range(LEVELS):
         above[l * BW : (l + 1) * BW, :] = field_of(ancestors[l, me], 1 + l)
-    total[...] = jnp.dot(coupling[...], above[...], preferred_element_type=F32)
+
+    def couple(b, c):
+        rows = pl.ds(pl.multiple_of(b * STEP, STEP), STEP)
+        total[rows, :] = jnp.dot(coupling[rows, :], above[...], preferred_element_type=F32)
+        return c
+
+    lax.fori_loop(0, PHYS // STEP, couple, 0)
     row = lax.broadcasted_iota(jnp.int32, (128, 256), 0)
     col = lax.broadcasted_iota(jnp.int32, (128, 256), 1)
     for g, (start, size, first, last) in enumerate(GROUPS):
@@ -263,13 +270,19 @@
             for r in range(1 + len(GROUPS)):
                 settle(send_b[r].at[pl.ds(0, N_SUB - 1)], send_b_sem.at[r])
         cols = slice(first * 128, last * 128)
-        part = total[...] + jnp.dot(
-            modes[:, cols], weights[cols, :], preferred_element_type=F32
-        )
-        if g < len(GROUPS) - 1:
-            total[...] = part
-        else:
-            out[...] = part.astype(BF16)
+
+        def finish(b, c):
+            rows = pl.ds(pl.multiple_of(b * STEP, STEP), STEP)
+            part = total[rows, :] + jnp.dot(
+                modes[rows, cols], weights[cols, :], preferred_element_type=F32
+            )
+            if g < len(GROUPS) - 1:
+                total[rows, :] = part
+            else:
+                out[rows, :] = part.astype(BF16)
+            return c
+
+        lax.fori_loop(0, PHYS // STEP, finish, 0)
 
 
 def store(interior, field, interior_out, field_out, sem):

time: 32.1 us -> 28.8 us (0.90)
  Pallas kernels: 31.4 us -> 28.1 us
    pallas_call x1, Pallas kernels: 30.4 us -> 27.1 us  [body(): pl.pallas_call(kernel, out_shape=(pltpu.VMEM((PHYS, 128), BF16), pltpu.VM...]
where the time goes in v4:
time: 28.8 us; the launch traced here: 28.7 us
  Pallas kernels  28.1 us (98%)
  between operations  0.64 us (2%)
    pallas_call x1, Pallas kernels, body(): pl.pallas_call(kernel, out_shape=(pltpu.VMEM((PHYS, 128), BF16), pltpu.VM...  27.1 us
    pallas_call x1, Pallas kernels, body(): pl.pallas_call(store, out_shape=tuple((jax.ShapeDtypeStruct((rows, 128),...  0.99 us

profile of v4, /device:TPU:1, one launch (start us, length us, event | category | flops | bytes accessed | tf_op | source)
XLA Modules:
  0.0 28.7 jit_solution(16498576650372628986)
XLA Ops:
  0.6 27.1 %recover.1 = (bf16[4096,128]{1,0:T(8,128)(2,1)S(1)}, bf16[256,128]{1,0:T(8,128)(2,1)S(1)}) custom-call(s32[32]{0:T(128)} %counts_hbm.1, s32[3,32]{1,0:T(4,128)} %bitcast.4, s32[3,1,16]{2,1,0:T(1,128)} %bitcast.5, bf16[32,2560]{1,0:T(8,128)(2,1)} %coef_hbm.1, bf16[4096,1024]{1,0:T(8,128)(2,1)} %modes_hbm.1, bf16[32,256,128]{2,1,0:T(8,128)(2,1)} %bitcast.3, ...), custom_call_target="tpu_custom_call" | custom-call | tf_op jit(solution)/shard_map/recover/pallas_call | solution.py:305
  27.7 1.0 %store.1 = (bf16[4096,128]{1,0:T(8,128)(2,1)}, bf16[256,128]{1,0:T(8,128)(2,1)}) custom-call(bf16[4096,128]{1,0:T(8,128)(2,1)S(1)} %get-tuple-element.4.interior, bf16[256,128]{1,0:T(8,128)(2,1)S(1)} %get-tuple-element.5.field), custom_call_target="tpu_custom_call" | custom-call | tf_op jit(solution)/shard_map/store/pallas_call | solution.py:347

commit v5 on v4

--- a/solution.py
+++ b/solution.py
@@ -15,9 +15,10 @@
 ROWS = 4
 TILES_A = 20
 TILES_I = 128
-SEPS = 1 + LEVELS
+SEPS = LEVELS + 1
 WIN = 9
-GROUPS = ((0, 5, 0, 4), (5, 4, 4, 8))
+GROUPS = ((0, 3), (3, 4), (7, 3), (10, 2))
+LAST = 6 * 128
 CAP = 1024
 PHYS = 4096
 NBLK = PHYS // BW
@@ -36,7 +37,9 @@
     modes_hbm,
     sep_hbm,
     coupling_hbm,
-    out,
+    total,
+    modes_last,
+    coef_last,
     field,
     counts,
     ancestors,
@@ -50,8 +53,6 @@
     recv_s,
     lanes,
     above,
-    total,
-    weights,
     load_sem,
     send_a_sem,
     recv_a_sem,
@@ -79,7 +80,8 @@
     load_coef = load(coef_hbm, coef, 0)
     load_sep = load(sep_hbm, sep, 1)
     load_coupling = load(coupling_hbm, coupling, 2)
-    load_modes = load(modes_hbm, modes, 3)
+    load_modes = load(modes_hbm.at[:, pl.ds(0, LAST)], modes, 3)
+    load_last = load(modes_hbm.at[:, pl.ds(LAST, CAP - LAST)], modes_last, 7)
     load_counts = load(counts_hbm, counts, 4)
     load_ancestors = load(ancestors_hbm, ancestors, 5)
     load_gates = load(gates_hbm, gates, 6)
@@ -99,6 +101,7 @@
     load_sep.start()
     load_coupling.start()
     load_modes.start()
+    load_last.start()
     load_coef.wait()
 
     def split_rows(t, c):
@@ -197,24 +200,33 @@
 
     settle(recv_s, recv_a_sem.at[0])
     for s in range(N_SUB):
-        send_b[0][s, 0] = recv_s[s]
+        send_b[1][s, 0] = recv_s[s]
         for l in range(LEVELS):
-            send_b[0][s, 1 + l] = recv_s[ancestors[l, s]]
+            send_b[0][s, l] = recv_s[ancestors[l, s]]
     send_group(0)
     settle(recv_i.at[pl.ds(0, TILES_I)], recv_a_sem.at[1])
     offset = jnp.int32(0)
-    my_off = jnp.int32(0)
+    starts = []
     for s in range(N_SUB):
-        for g, (start, size, _, _) in enumerate(GROUPS):
-            send_b[1 + g][s] = recv_i[pl.ds((offset >> 7) + start, size)]
-        my_off = my_off + jnp.where(s < me, counts[s], 0)
+        starts.append(offset)
         offset = offset + counts[s]
-    for g in range(len(GROUPS)):
-        send_group(1 + g)
-    my_count = counts[me]
-    shift = my_off & 127
-
-    def gather(g, start, size):
+    for g in range(1, len(GROUPS)):
+        skip = 1 if g == 1 else 0
+        first = GROUPS[g][0] + skip - SEPS
+        size = GROUPS[g][1] - skip
+        lane = lax.broadcasted_iota(jnp.int32, (size, ROWS, 128), 2)
+        place = lane + 128 * (first + lax.broadcasted_iota(jnp.int32, (size, ROWS, 128), 0))
+        for s in range(N_SUB):
+            shift = starts[s] & 127
+            tiles = recv_i[pl.ds((starts[s] >> 7) + first, size + 1)].astype(F32)
+            turned = pltpu.roll(tiles, (128 - shift) & 127, 2)
+            window = jnp.where(lane < 128 - shift, turned[:size], turned[1:])
+            window = jnp.where(place < counts[s], window, 0.0)
+            send_b[g][s, skip:] = window.astype(BF16)
+        send_group(g)
+
+    def gather(g):
+        start, size = GROUPS[g]
         settle(recv_b[g], recv_b_sem.at[g])
 
         def step(k, c):
@@ -239,16 +251,16 @@
     lax.fori_loop(0, NBLK, mask, 0)
     load_sep.wait()
     load_modes.wait()
+    load_last.wait()
     settle(send_a.at[pl.ds(0, N_VEC - 1)], send_a_sem.at[0])
-    gather(0, 0, SEPS)
+    gather(0)
 
     def field_of(index, t):
         block = lanes[:, :, t * 128 : (t + 1) * 128].reshape(128, 128)
         return lax.dot_general(sep[index], block, NT, preferred_element_type=F32).astype(BF16)
 
-    field[...] = field_of(me, 0)
     for l in range(LEVELS):
-        above[l * BW : (l + 1) * BW, :] = field_of(ancestors[l, me], 1 + l)
+        above[l * BW : (l + 1) * BW, :] = field_of(ancestors[l, me], l)
 
     def couple(b, c):
         rows = pl.ds(pl.multiple_of(b * STEP, STEP), STEP)
@@ -256,73 +268,89 @@
         return c
 
     lax.fori_loop(0, PHYS // STEP, couple, 0)
-    row = lax.broadcasted_iota(jnp.int32, (128, 256), 0)
-    col = lax.broadcasted_iota(jnp.int32, (128, 256), 1)
-    for g, (start, size, first, last) in enumerate(GROUPS):
-        gather(1 + g, SEPS + start, size)
-        for t in range(first, last):
-            pick = jnp.where((col == row + shift) & (row + t * 128 < my_count), 1.0, 0.0)
-            pair = lanes[:, :, (SEPS + t) * 128 : (SEPS + t + 2) * 128].reshape(128, 256)
-            weights[t * 128 : (t + 1) * 128, :] = lax.dot_general(
-                pick.astype(BF16), pair, NT, preferred_element_type=F32
-            ).astype(BF16)
-        if g == len(GROUPS) - 1:
-            for r in range(1 + len(GROUPS)):
-                settle(send_b[r].at[pl.ds(0, N_SUB - 1)], send_b_sem.at[r])
-        cols = slice(first * 128, last * 128)
-
-        def finish(b, c):
+    for g in range(1, len(GROUPS) - 1):
+        gather(g)
+        first, size = GROUPS[g]
+        if g == 1:
+            field[...] = field_of(me, LEVELS)
+            first, size = first + 1, size - 1
+        wide = slice(first * 128, (first + size) * 128)
+        cols = slice((first - SEPS) * 128, (first - SEPS + size) * 128)
+
+        def add(b, c):
             rows = pl.ds(pl.multiple_of(b * STEP, STEP), STEP)
-            part = total[rows, :] + jnp.dot(
-                modes[rows, cols], weights[cols, :], preferred_element_type=F32
+            total[rows, :] = total[rows, :] + lax.dot_general(
+                modes[rows, cols],
+                lanes[:, :, wide].reshape(128, wide.stop - wide.start),
+                NT,
+                preferred_element_type=F32,
             )
-            if g < len(GROUPS) - 1:
-                total[rows, :] = part
-            else:
-                out[rows, :] = part.astype(BF16)
             return c
 
-        lax.fori_loop(0, PHYS // STEP, finish, 0)
-
-
-def store(interior, field, interior_out, field_out, sem):
-    copies = (
-        pltpu.make_async_copy(interior, interior_out, sem.at[0]),
-        pltpu.make_async_copy(field, field_out, sem.at[1]),
-    )
-    for copy in copies:
-        copy.start()
-    for copy in copies:
-        copy.wait()
+        lax.fori_loop(0, PHYS // STEP, add, 0)
+    gather(len(GROUPS) - 1)
+    coef_last[...] = lanes[:, :, SEPS * 128 + LAST :].reshape(128, CAP - LAST)
+    for g in range(len(GROUPS)):
+        settle(send_b[g].at[pl.ds(0, N_SUB - 1)], send_b_sem.at[g])
+
+
+def finish(total, modes, coef, field, interior_out, field_out, interior, sem, field_sem):
+    store_field = pltpu.make_async_copy(field, field_out, field_sem.at[0])
+    store_field.start()
+
+    def rows_of(b):
+        return pl.ds(pl.multiple_of(b * STEP, STEP), STEP)
+
+    def store(b):
+        return pltpu.make_async_copy(
+            interior.at[rows_of(b)], interior_out.at[rows_of(b)], sem.at[b]
+        )
+
+    def step(b, c):
+        rows = rows_of(b)
+        part = total[rows, :] + lax.dot_general(
+            modes[rows, :], coef[...], NT, preferred_element_type=F32
+        )
+        interior[rows, :] = part.astype(BF16)
+        store(b).start()
+        return c
+
+    lax.fori_loop(0, PHYS // STEP, step, 0)
+    store_field.wait()
+    for b in range(PHYS // STEP):
+        store(b).wait()
 
 
 def body(coefficients, row_counts, ancestors, interior_modes, separator_modes, coupling, pattern):
     hbm = pl.BlockSpec(memory_space=pl.ANY)
     vmem = pl.BlockSpec(memory_space=pltpu.VMEM)
     dma = pltpu.SemaphoreType.DMA
-    sizes = [SEPS] + [size for _, size, _, _ in GROUPS]
+    sizes = [size for _, size in GROUPS]
     slots = [pltpu.VMEM((N_SUB, size, ROWS, 128), BF16) for size in sizes]
     results = pl.pallas_call(
         kernel,
-        out_shape=(pltpu.VMEM((PHYS, 128), BF16), pltpu.VMEM((BW, 128), BF16)),
+        out_shape=(
+            pltpu.VMEM((PHYS, 128), F32),
+            pltpu.VMEM((PHYS, CAP - LAST), BF16),
+            pltpu.VMEM((128, CAP - LAST), BF16),
+            pltpu.VMEM((BW, 128), BF16),
+        ),
         in_specs=[hbm] * 7,
-        out_specs=(vmem, vmem),
+        out_specs=(vmem,) * 4,
         scratch_shapes=[
             pltpu.SMEM((N_SUB,), jnp.int32),
             pltpu.SMEM((LEVELS, N_SUB), jnp.int32),
             pltpu.SMEM((LEVELS, 1, NBLK), jnp.int32),
             pltpu.VMEM((ROWS * N_VEC, TILES_A * 128), BF16),
-            pltpu.VMEM((PHYS, CAP), BF16),
+            pltpu.VMEM((PHYS, LAST), BF16),
             pltpu.VMEM((N_SUB, BW, SEPM), BF16),
             pltpu.VMEM((PHYS, LEVELS * BW), BF16),
             pltpu.VMEM((N_VEC, TILES_A, ROWS, 128), BF16),
             pltpu.VMEM((TILES_I + WIN - 1, ROWS, 128), BF16),
             pltpu.VMEM((N_SUB, ROWS, 128), BF16),
-            pltpu.VMEM((N_SUB // 4, 4 * ROWS, (SEPS + WIN) * 128), BF16),
+            pltpu.VMEM((N_SUB // 4, 4 * ROWS, SEPS * 128 + CAP), BF16),
             pltpu.VMEM((LEVELS * BW, 128), BF16),
-            pltpu.VMEM((PHYS, 128), F32),
-            pltpu.VMEM((CAP, 128), BF16),
-            dma((7,)),
+            dma((8,)),
             dma((1,)),
             dma((2,)),
             dma((len(sizes),)),
@@ -332,26 +360,31 @@
             *slots,
         ],
         compiler_params=pltpu.CompilerParams(
-            collective_id=0, has_side_effects=True, vmem_limit_bytes=60 * 1024 * 1024
+            collective_id=0, has_side_effects=True, vmem_limit_bytes=48 * 1024 * 1024
         ),
         name="recover",
     )(
-        row_counts,
-        ancestors.T,
-        jnp.transpose(pattern, (2, 0, 1)),
-        coefficients,
-        interior_modes,
-        separator_modes.reshape(N_SUB, BW, SEPM),
-        coupling,
+        *[
+            pltpu.with_memory_space_constraint(x, pltpu.HBM)
+            for x in (
+                row_counts,
+                ancestors.T,
+                jnp.transpose(pattern, (2, 0, 1)),
+                coefficients,
+                interior_modes,
+                separator_modes.reshape(N_SUB, BW, SEPM),
+                coupling,
+            )
+        ]
     )
     return pl.pallas_call(
-        store,
+        finish,
         out_shape=tuple(jax.ShapeDtypeStruct((rows, 128), BF16) for rows in (PHYS, BW)),
-        in_specs=[vmem] * 2,
+        in_specs=[vmem] * 4,
         out_specs=(hbm, hbm),
-        scratch_shapes=[dma((2,))],
+        scratch_shapes=[pltpu.VMEM((PHYS, 128), BF16), dma((PHYS // STEP,)), dma((1,))],
         compiler_params=pltpu.CompilerParams(vmem_limit_bytes=8 * 1024 * 1024),
-        name="store",
+        name="finish",
     )(*[pltpu.with_memory_space_constraint(x, pltpu.VMEM) for x in results])
 
 

time: 28.8 us -> 27.6 us (0.958)
  Pallas kernels: 28.1 us -> 26.9 us
    pallas_call x2, Pallas kernels: 28.1 us -> 26.9 us  [the longest x1 25.2 us: body(): pl.pallas_call(kernel, out_shape=(pltpu.VMEM((PHYS, 128), F32), pltpu.VME...]
where the time goes in v5:
time: 27.6 us; the launch traced here: 27.5 us
  Pallas kernels  26.9 us (97%)
  between operations  0.64 us (2%)
    pallas_call x1, Pallas kernels, body(): pl.pallas_call(kernel, out_shape=(pltpu.VMEM((PHYS, 128), F32), pltpu.VME...  25.2 us
    pallas_call x1, Pallas kernels, body(): pl.pallas_call(finish, out_shape=tuple((jax.ShapeDtypeStruct((rows, 128),...  1.68 us

profile of v5, /device:TPU:1, one launch (start us, length us, event | category | flops | bytes accessed | tf_op | source)
XLA Modules:
  0.0 27.5 jit_solution(15547464109803591842)
XLA Ops:
  0.6 25.2 %recover.1 = (f32[4096,128]{1,0:T(8,128)S(1)}, bf16[4096,256]{1,0:T(8,128)(2,1)S(1)}, bf16[128,256]{1,0:T(8,128)(2,1)S(1)}, bf16[256,128]{1,0:T(8,128)(2,1)S(1)}) custom-call(s32[32]{0:T(128)} %counts_hbm.1, s32[3,32]{1,0:T(4,128)} %bitcast.4, s32[3,1,16]{2,1,0:T(1,128)} %bitcast.5, bf16[32,2560]{1,0:T(8,128)(2,1)} %coef_hbm.1, ...), custom_call_target="tpu_custom_call" | custom-call | tf_op jit(solution)/shard_map/recover/pallas_call | solution.py:330
  25.9 1.7 %finish.1 = (bf16[4096,128]{1,0:T(8,128)(2,1)}, bf16[256,128]{1,0:T(8,128)(2,1)}) custom-call(f32[4096,128]{1,0:T(8,128)S(1)} %get-tuple-element.6.total, bf16[4096,256]{1,0:T(8,128)(2,1)S(1)} %get-tuple-element.7.modes, bf16[128,256]{1,0:T(8,128)(2,1)S(1)} %get-tuple-element.8.coef, bf16[256,128]{1,0:T(8,128)(2,1)S(1)} %get-tuple-element.9.field), custom_call_target="tpu_custom_call" | custom-call | tf_op jit(solution)/shard_map/finish/pallas_call | solution.py:380

commit v6 on v5

--- a/solution.py
+++ b/solution.py
@@ -175,11 +175,13 @@
     pl.semaphore_wait(relay_sem.at[4], 1)
 
     def send_group(g):
-        def row(j, xs):
+        def place(j):
             h = lax.div(j + 1, 2)
-            dz = 4 + h * (1 - 2 * lax.rem(j, 2))
-            z = lax.rem(mz + dz, N_Z)
-            for dx in xs:
+            dz = (1 - 2 * lax.rem(mv, 2)) * h * (1 - 2 * lax.rem(j, 2))
+            return lax.rem(mz + 12 + dz, N_Z)
+
+        def send(z, dxs):
+            for dx in dxs:
                 s = lax.rem(mx + dx, N_X) * N_Z + z
                 pltpu.make_async_remote_copy(
                     src_ref=send_b[g].at[s],
@@ -191,11 +193,11 @@
                 ).start()
 
         def step(j, c):
-            row(j, range(N_X))
+            send(place(j), (2, 1, 3, 0))
             return c
 
-        lax.fori_loop(0, N_Z - 1, step, 0)
-        row(N_Z - 1, range(1, N_X))
+        lax.fori_loop(0, 7, step, 0)
+        send(mz, (2, 1, 3))
         pltpu.make_async_copy(send_b[g].at[me], recv_b[g].at[me], recv_b_sem.at[g]).start()
 
     settle(recv_s, recv_a_sem.at[0])

time: 27.6 us -> 27.2 us (0.986)
  Pallas kernels: 26.9 us -> 26.5 us
    pallas_call x1, Pallas kernels: 25.2 us -> 24.8 us  [body(): pl.pallas_call(kernel, out_shape=(pltpu.VMEM((PHYS, 128), F32), pltpu.VME...]
where the time goes in v6:
time: 27.2 us
  Pallas kernels  26.5 us (97%)
  between operations  0.64 us (2%)
    pallas_call x1, Pallas kernels, body(): pl.pallas_call(kernel, out_shape=(pltpu.VMEM((PHYS, 128), F32), pltpu.VME...  24.8 us
    pallas_call x1, Pallas kernels, body(): pl.pallas_call(finish, out_shape=tuple((jax.ShapeDtypeStruct((rows, 128),...  1.69 us

profile of v6, /device:TPU:1, one launch (start us, length us, event | category | flops | bytes accessed | tf_op | source)
XLA Modules:
  0.0 27.2 jit_solution(730992302318285535)
XLA Ops:
  0.6 24.8 %recover.1 = (f32[4096,128]{1,0:T(8,128)S(1)}, bf16[4096,256]{1,0:T(8,128)(2,1)S(1)}, bf16[128,256]{1,0:T(8,128)(2,1)S(1)}, bf16[256,128]{1,0:T(8,128)(2,1)S(1)}) custom-call(s32[32]{0:T(128)} %counts_hbm.1, s32[3,32]{1,0:T(4,128)} %bitcast.4, s32[3,1,16]{2,1,0:T(1,128)} %bitcast.5, bf16[32,2560]{1,0:T(8,128)(2,1)} %coef_hbm.1, ...), custom_call_target="tpu_custom_call" | custom-call | tf_op jit(solution)/shard_map/recover/pallas_call | solution.py:332
  25.5 1.7 %finish.1 = (bf16[4096,128]{1,0:T(8,128)(2,1)}, bf16[256,128]{1,0:T(8,128)(2,1)}) custom-call(f32[4096,128]{1,0:T(8,128)S(1)} %get-tuple-element.6.total, bf16[4096,256]{1,0:T(8,128)(2,1)S(1)} %get-tuple-element.7.modes, bf16[128,256]{1,0:T(8,128)(2,1)S(1)} %get-tuple-element.8.coef, bf16[256,128]{1,0:T(8,128)(2,1)S(1)} %get-tuple-element.9.field), custom_call_target="tpu_custom_call" | custom-call | tf_op jit(solution)/shard_map/finish/pallas_call | solution.py:382

commit v7 on v6

--- a/solution.py
+++ b/solution.py
@@ -98,10 +98,6 @@
     load_counts.start()
     load_ancestors.start()
     load_gates.start()
-    load_sep.start()
-    load_coupling.start()
-    load_modes.start()
-    load_last.start()
     load_coef.wait()
 
     def split_rows(t, c):
@@ -162,6 +158,10 @@
     def settle(ref, sem):
         pltpu.make_async_copy(ref, ref, sem).wait()
 
+    load_sep.start()
+    load_coupling.start()
+    load_modes.start()
+    load_last.start()
     load_counts.wait()
     load_ancestors.wait()
     load_gates.wait()

time: 27.2 us -> 27.3 us (level)
  no operation moved by 1% of the time
where the time goes in v7:
time: 27.3 us; the launch traced here: 27.2 us
  Pallas kernels  26.5 us (97%)
  between operations  0.64 us (2%)
    pallas_call x1, Pallas kernels, body(): pl.pallas_call(kernel, out_shape=(pltpu.VMEM((PHYS, 128), F32), pltpu.VME...  24.8 us
    pallas_call x1, Pallas kernels, body(): pl.pallas_call(finish, out_shape=tuple((jax.ShapeDtypeStruct((rows, 128),...  1.69 us

profile of v7, /device:TPU:1, one launch (start us, length us, event | category | flops | bytes accessed | tf_op | source)
XLA Modules:
  0.0 27.2 jit_solution(12120371234045857065)
XLA Ops:
  0.6 24.8 %recover.1 = (f32[4096,128]{1,0:T(8,128)S(1)}, bf16[4096,256]{1,0:T(8,128)(2,1)S(1)}, bf16[128,256]{1,0:T(8,128)(2,1)S(1)}, bf16[256,128]{1,0:T(8,128)(2,1)S(1)}) custom-call(s32[32]{0:T(128)} %counts_hbm.1, s32[3,32]{1,0:T(4,128)} %bitcast.4, s32[3,1,16]{2,1,0:T(1,128)} %bitcast.5, bf16[32,2560]{1,0:T(8,128)(2,1)} %coef_hbm.1, ...), custom_call_target="tpu_custom_call" | custom-call | tf_op jit(solution)/shard_map/recover/pallas_call | solution.py:332
  25.5 1.7 %finish.1 = (bf16[4096,128]{1,0:T(8,128)(2,1)}, bf16[256,128]{1,0:T(8,128)(2,1)}) custom-call(f32[4096,128]{1,0:T(8,128)S(1)} %get-tuple-element.6.total, bf16[4096,256]{1,0:T(8,128)(2,1)S(1)} %get-tuple-element.7.modes, bf16[128,256]{1,0:T(8,128)(2,1)S(1)} %get-tuple-element.8.coef, bf16[256,128]{1,0:T(8,128)(2,1)S(1)} %get-tuple-element.9.field), custom_call_target="tpu_custom_call" | custom-call | tf_op jit(solution)/shard_map/finish/pallas_call | solution.py:382
